TPU v7x, 512 devices: a whole 4x4x16 slice. The times are simulated.
512 devices in a mesh: pipe: 8 (over x_hi, y), expert: 64 (over z, x_lo, core).
Axes of the slice: x: 4 (x_hi: 2, x_lo: 2; x = x_hi * 2 + x_lo), y: 4, z: 16, core: 2. Of those that a mesh axis runs over, the one named last changes fastest.
Arguments:
- activations: bfloat16 [8, 768, 3584], P('pipe', 'expert'), may hold values from -6 to 6
- out_grads: bfloat16 [8, 768, 3584], P('pipe', 'expert'), may hold values from -6 to 6
- gate_vals: float32 [8, 768, 8], P('pipe', 'expert'), may hold values from 0.05 to 0.3
- routes: int32 [8, 768, 8], P('pipe', 'expert'), may hold values from 0 to 15, all different within a row; in each aligned block of 12 rows (0 to 11, 12 to 23, ..., all dimensions but the last counted through in order) at most 9 rows name the same one
- up_weight: bfloat16 [8, 3584, 16384], P('pipe', None, 'expert'), may hold values from -0.09375 to 0.09375
- down_weight: bfloat16 [8, 16384, 3584], P('pipe', 'expert'), may hold values from -0.1875 to 0.1875
Outputs:
- handed_grads: bfloat16 [8, 768, 3584], P('pipe', 'expert')
- gate_grads: float32 [8, 768, 8], P('pipe', 'expert')
Inputs may be any that keep to these rules, and one draw needn't show every extreme that they name: `routes`: each token names 8 different experts; among the 12 tokens of one device at most 9 name the same expert, and on some device some expert is named by exactly 9 of them.
All inputs are finite; a program needn't handle non-finite values.
Results may differ from a plain program's by a relative error of at most 0.008.
Values may be sent and summed in bfloat16 or wider, within the bound.
No kernel may reach another device: no remote copies, remote signals or barrier semaphores. Data moves between devices by JAX's collectives and lax.ppermute only.
A program may use at most 128 MiB of HBM per device.

v0:
```python
import jax
import jax.numpy as jnp
from jax import lax
from jax.sharding import PartitionSpec as P

EXPERTS = 16
CAP = 9


def from_behind(block, axis, distance):
    devices = range(lax.axis_size(axis))
    route = [(i - distance, i) for i in devices if i - distance in devices]
    return lax.ppermute(block, axis, route)


def on_device(activations, out_grads, gate_vals, routes, up_weight, down_weight):
    highest = lax.Precision.HIGHEST
    inputs = activations[0]
    upstream = out_grads[0]
    section_gates = gate_vals[0]
    section_routes = routes[0]
    local_up = up_weight[0]
    local_down = down_weight[0]
    tok_count, model_width = inputs.shape
    devices = lax.axis_size("expert")
    group_size = devices // EXPERTS
    onehot = (
        section_routes[:, :, None] == jnp.arange(EXPERTS, dtype=jnp.int32)[None, None, :]
    ).astype(jnp.float32)
    picked = jnp.sum(onehot, axis=1)
    slot_index = jnp.cumsum(picked, axis=0) - 1.0
    slot_hits = slot_index.T[:, None, :] == jnp.arange(CAP, dtype=jnp.float32)[None, :, None]
    slot_map = picked.T[:, None, :] * slot_hits.astype(jnp.float32)
    slot_bf = slot_map.astype(jnp.bfloat16)
    expert_gate = jnp.einsum("tke,tk->et", onehot, section_gates, precision=highest)
    weighted_map = slot_map * expert_gate[:, None, :]
    sent_in = jnp.einsum("ect,td->ecd", slot_bf, inputs, preferred_element_type=jnp.float32).astype(
        jnp.bfloat16
    )
    sent_up = jnp.einsum(
        "ect,td->ecd", slot_bf, upstream, preferred_element_type=jnp.float32
    ).astype(jnp.bfloat16)
    sent_in = jnp.broadcast_to(sent_in[:, None], (EXPERTS, group_size, CAP, model_width)).reshape(
        devices, CAP, model_width
    )
    sent_up = jnp.broadcast_to(sent_up[:, None], (EXPERTS, group_size, CAP, model_width)).reshape(
        devices, CAP, model_width
    )
    got_in, got_up = (
        lax.all_to_all(sent_in, "expert", split_axis=0, concat_axis=0, tiled=True),
        lax.all_to_all(sent_up, "expert", split_axis=0, concat_axis=0, tiled=True),
    )
    in_rows = got_in.reshape(devices * CAP, model_width)
    up_rows = got_up.reshape(devices * CAP, model_width)
    pre_act = jnp.dot(in_rows, local_up, preferred_element_type=jnp.float32)
    hid_grad = lax.dot_general(
        up_rows, local_down, (((1,), (1,)), ((), ())), preferred_element_type=jnp.float32
    )
    sig_val = jax.nn.sigmoid(pre_act)
    silu_val = pre_act * sig_val
    silu_slope = sig_val * (1.0 + pre_act * (1.0 - sig_val))
    act_grad = (hid_grad * silu_slope).astype(jnp.bfloat16)
    partial_dx = lax.dot_general(
        act_grad, local_up, (((1,), (1,)), ((), ())), preferred_element_type=jnp.float32
    )
    partial_dx = partial_dx.reshape(devices, CAP, model_width)
    partial_dg = jnp.sum(hid_grad * silu_val, axis=1).reshape(devices, CAP)
    returned, returned_dg = (
        lax.all_to_all(partial_dx, "expert", split_axis=0, concat_axis=0, tiled=True),
        lax.all_to_all(partial_dg, "expert", split_axis=0, concat_axis=0, tiled=True),
    )
    summed = jnp.sum(returned.reshape(EXPERTS, group_size, CAP, model_width), axis=1)
    input_grad = jnp.einsum("ect,ecd->td", weighted_map, summed, precision=highest)
    expert_dg = jnp.sum(returned_dg.reshape(EXPERTS, group_size, CAP), axis=1)
    token_dg = jnp.einsum("ect,ec->et", slot_map, expert_dg, precision=highest)
    gate_grad = jnp.einsum("tke,et->tk", onehot, token_dg, precision=highest)
    grad_bf = input_grad.astype(jnp.bfloat16)
    handed = from_behind(grad_bf[None], "pipe", -1)
    return (handed, gate_grad[None])


def solution(mesh):
    placed = (
        P("pipe", "expert", None),
        P("pipe", "expert", None),
        P("pipe", "expert", None),
        P("pipe", "expert", None),
        P("pipe", None, "expert"),
        P("pipe", "expert", None),
    )
    return jax.shard_map(
        on_device,
        mesh=mesh,
        in_specs=placed,
        out_specs=(P("pipe", "expert", None), P("pipe", "expert", None)),
        check_vma=False,
    )
```

profile of v0, /device:TPU:24, one launch (start us, length us, event | category | flops | bytes accessed | tf_op | source)
XLA Modules:
  0.0 1396.1 jit_solution(3252933490257129475)
XLA Ops:
  0.6 0.0 copy-start
  0.6 0.9 copy.37
  1.5 0.1 convert_reduce_fusion
  1.7 1.3 convolution_convert_fusion
  3.0 0.6 copy.41
  3.7 4.0 broadcast_in_dim.9
  7.6 0.0 copy-start.2
  7.6 17.4 %all-to-all-start.1 = ((bf16[64,9,3584]{2,1,0:T(8,128)(2,1)}), bf16[64,9,3584]{2,1,0:T(8,128)(2,1)}, u32[]{:S(2)}, u32[]{:S(2)}) async-start(bf16[64,9,3584]{2,1,0:T(8,128)(2,1)} %bitcast.62), calls=%async_computation.1 | async-start | bytes 14680064 | tf_op jit(solution)/shard_map/all_to_all | solution.py:50
  25.0 0.0 copy-done.2
  25.1 0.4 convolution_convert_fusion.1
  25.5 1.9 copy.39
  27.4 323.3 %all-to-all-done.1 = bf16[64,9,3584]{2,1,0:T(8,128)(2,1)} async-done(((bf16[64,9,3584]{2,1,0:T(8,128)(2,1)}), bf16[64,9,3584]{2,1,0:T(8,128)(2,1)}, u32[]{:S(2)}, u32[]{:S(2)}) %all-to-all-start.1) | async-done | bytes 4128800 | tf_op jit(solution)/shard_map/all_to_all | solution.py:50
  350.7 5.3 broadcast_in_dim.8
  356.0 5.7 all-to-all-start
  361.7 8.0 reshape.38
  369.8 0.0 copy-done
  369.8 3.4 fusion.5
  373.2 314.2 %all-to-all-done = bf16[64,9,3584]{2,1,0:T(8,128)(2,1)} async-done(((bf16[64,9,3584]{2,1,0:T(8,128)(2,1)}), bf16[64,9,3584]{2,1,0:T(8,128)(2,1)}, u32[]{:S(2)}, u32[]{:S(2)}) %all-to-all-start) | async-done | bytes 4128800 | tf_op jit(solution)/shard_map/all_to_all | solution.py:51
  687.4 7.9 reshape.36
  695.3 4.2 multiply_reduce_fusion
  699.5 0.8 all_to_all.18
  700.3 4.8 all-to-all-start.3
  705.0 0.1 dot_general.34
  705.2 1.3 fusion.3
  706.5 10.4 copy.43
  716.9 0.0 copy-start.3
  716.9 1.3 all-to-all-done.3
  718.1 12.7 all-to-all-start.2
  730.9 0.0 copy-done.3
  730.9 0.1 copy.46
  731.0 0.2 fusion.17
  731.2 0.1 copy.50
  731.4 0.3 fusion.34
  731.7 0.1 copy.59
  731.8 639.1 %all-to-all-done.2 = f32[64,9,3584]{2,1,0:T(8,128)} async-done(((f32[64,9,3584]{2,1,0:T(8,128)}), f32[64,9,3584]{2,1,0:T(8,128)}, u32[]{:S(2)}, u32[]{:S(2)}) %all-to-all-start.2) | async-done | bytes 8257568 | tf_op jit(solution)/shard_map/all_to_all | solution.py:69
  1370.9 0.0 copy-start.1
  1370.9 9.1 bitcast_reduce_fusion
  1380.0 5.2 fusion.1
  1385.2 2.7 collective-permute-start
  1387.8 0.2 select_reduce_fusion
  1388.0 0.7 copy.58
  1388.7 6.8 collective-permute-done
  1395.5 0.6 copy.67
  1396.1 0.0 copy-done.1
  (5 shorter events, 0.1 us)
Async XLA Ops:
  0.6 369.1 %copy-start = (bf16[1,3584,256]{2,1,0:T(8,128)(2,1)S(1)}, bf16[1,3584,256]{2,1,0:T(8,128)(2,1)}, u32[]{:S(2)}) copy-start(bf16[1,3584,256]{2,1,0:T(8,128)(2,1)} %param.10) | copy-start | bytes 5505028
  7.6 17.4 %copy-start.2 = (bf16[1,12,3584]{2,1,0:T(8,128)(2,1)S(1)}, bf16[1,12,3584]{2,1,0:T(8,128)(2,1)}, u32[]{:S(2)}) copy-start(bf16[1,12,3584]{2,1,0:T(8,128)(2,1)} %param.7) | copy-start | bytes 258052
  7.6 343.0 %all-to-all-start.1 = ((bf16[64,9,3584]{2,1,0:T(8,128)(2,1)}), bf16[64,9,3584]{2,1,0:T(8,128)(2,1)}, u32[]{:S(2)}, u32[]{:S(2)}) async-start(bf16[64,9,3584]{2,1,0:T(8,128)(2,1)} %bitcast.62), calls=%async_computation.1 | async-start | bytes 14680064 | tf_op jit(solution)/shard_map/all_to_all | solution.py:50
  356.0 331.4 %all-to-all-start = ((bf16[64,9,3584]{2,1,0:T(8,128)(2,1)}), bf16[64,9,3584]{2,1,0:T(8,128)(2,1)}, u32[]{:S(2)}, u32[]{:S(2)}) async-start(bf16[64,9,3584]{2,1,0:T(8,128)(2,1)} %bitcast.61), calls=%async_computation | async-start | bytes 14680064 | tf_op jit(solution)/shard_map/all_to_all | solution.py:51
  700.3 17.9 %all-to-all-start.3 = ((f32[64,1,9]{2,1,0:T(1,128)}), f32[64,1,9]{2,1,0:T(1,128)S(1)}, u32[]{:S(2)}, u32[]{:S(2)}) async-start(f32[64,1,9]{2,1,0:T(1,128)} %bitcast.21), calls=%async_computation.3 | async-start | bytes 65536 | tf_op jit(solution)/shard_map/all_to_all | solution.py:70
  716.9 14.0 %copy-start.3 = (f32[1,12,8]{1,2,0:T(8,128)S(1)}, f32[1,12,8]{1,2,0:T(8,128)}, u32[]{:S(2)}) copy-start(f32[1,12,8]{1,2,0:T(8,128)} %param.8) | copy-start | bytes 1156
  718.1 652.8 %all-to-all-start.2 = ((f32[64,9,3584]{2,1,0:T(8,128)}), f32[64,9,3584]{2,1,0:T(8,128)}, u32[]{:S(2)}, u32[]{:S(2)}) async-start(f32[64,9,3584]{2,1,0:T(8,128)} %copy.43), calls=%async_computation.2 | async-start | bytes 29360128 | tf_op jit(solution)/shard_map/all_to_all | solution.py:69
  1370.9 25.2 %copy-start.1 = (bf16[1,3584,256]{2,1,0:T(8,128)(2,1)S(1)}, bf16[1,3584,256]{2,1,0:T(8,128)(2,1)}, u32[]{:S(2)}) copy-start(bf16[1,3584,256]{2,1,0:T(8,128)(2,1)} %param.10) | copy-start | bytes 5505028
  1385.2 10.3 collective-permute-start
where the time goes:
time: 1400 us
  waiting for transfers between devices  1280 us (91%)
  starting transfers between devices  43.3 us (3%)
  local copies, waits for them, and re-layouts  41.7 us (3%)
  matrix products  16.3 us (1%)
    all_to_all x1, waiting for transfers between devices, on_device(): lax.all_to_all(partial_dx, 'expert', split_axis=0, concat_axis=0, tiled=T...  639 us
    all_to_all x1, waiting for transfers between devices, on_device(): lax.all_to_all(sent_in, 'expert', split_axis=0, concat_axis=0, tiled=True)  323 us
    all_to_all x1, waiting for transfers between devices, on_device(): lax.all_to_all(sent_up, 'expert', split_axis=0, concat_axis=0, tiled=True)  314 us
  transfers between devices with their start and end apart: 5, of which 5 were waited for; matrix products, arithmetic and copies ran while one was open for 2% of the time, Pallas kernels for 0%

commit v1 on v0

v1 whole, which is shorter than its diff:
```python
import jax
import jax.numpy as jnp
from jax import lax
from jax.sharding import Mesh
from jax.sharding import PartitionSpec as P

EXPERTS = 16
COLUMN = ("z", "xl")
LANES = 128


def swap(block):
    return lax.ppermute(block, "c", [(0, 1), (1, 0)])


def pieces(values):
    high = values.astype(jnp.bfloat16)
    rest = values - high.astype(jnp.float32)
    middle = rest.astype(jnp.bfloat16)
    low = (rest - middle.astype(jnp.float32)).astype(jnp.bfloat16)
    return high, middle, low


def on_device(activations, out_grads, gate_vals, routes, up_weight, down_weight):
    inputs, upstream = activations[0], out_grads[0]
    gates, chosen = gate_vals[0], routes[0]
    local_up, local_down = up_weight[0], down_weight[0]
    tok, width = inputs.shape
    columns = lax.axis_size("z") * lax.axis_size("xl")
    core = lax.axis_index("c")
    first = core == 0
    expert = lax.axis_index("z")
    half = lax.axis_index("xl")

    onehot = (chosen[:, :, None] == jnp.arange(EXPERTS, dtype=jnp.int32)).astype(jnp.float32)
    dense = jnp.sum(onehot * gates[:, :, None], axis=1)
    tail = jnp.concatenate(pieces(dense), axis=1)
    tail = jnp.pad(tail, ((0, 0), (0, LANES - tail.shape[1])))

    keep = jnp.where(first, inputs, upstream)
    give = jnp.where(first, upstream, inputs)
    got = swap(jnp.concatenate([give, tail], axis=1))
    mine = jnp.concatenate([keep, tail], axis=1)
    block = jnp.concatenate([jnp.where(first, mine, got), jnp.where(first, got, mine)], axis=0)
    every = lax.all_gather(block, COLUMN, axis=0, tiled=True)

    up_rows = local_up.T
    other_up = swap(up_rows)
    both_up = jnp.concatenate(
        [jnp.where(first, up_rows, other_up), jnp.where(first, other_up, up_rows)], axis=0
    )
    other_down = lax.ppermute(local_down, "c", [(0, 1)])
    both_down = jnp.concatenate([other_down, local_down], axis=0)
    weights = jnp.where(first, both_up, both_down)

    raw = lax.dot_general(
        every[:, :width], weights, (((1,), (1,)), ((), ())), preferred_element_type=jnp.float32
    )
    hidden = raw.shape[1]
    raw = raw.reshape(columns, 2, tok, hidden)
    own = jnp.where(first, raw[:, 0], raw[:, 1]).reshape(columns * tok, hidden)
    other = jnp.where(first, raw[:, 1], raw[:, 0]).reshape(columns * tok, hidden)
    back = swap(other)
    pre_act = jnp.where(first, own, back)
    hid_grad = jnp.where(first, back, own)
    sig_val = jax.nn.sigmoid(pre_act)
    act_grad = (hid_grad * (sig_val * (1.0 + pre_act * (1.0 - sig_val)))).astype(jnp.bfloat16)
    partial_dg = jnp.sum(hid_grad * (pre_act * sig_val), axis=1)

    tails = every.reshape(columns, 2, tok, -1)[..., width:]
    tails = jnp.where(first, tails[:, 0], tails[:, 1]).reshape(columns * tok, LANES)
    lane = jnp.arange(LANES)
    named = ((lane % EXPERTS == expert) & (lane < 3 * EXPERTS)).astype(jnp.float32)
    weight = jnp.sum(tails.astype(jnp.float32) * named, axis=1)

    partial_dx = jnp.dot(act_grad, both_up, preferred_element_type=jnp.float32) * weight[:, None]
    slot = (lane == expert).astype(jnp.float32)
    packed = jnp.concatenate([partial_dx, partial_dg[:, None] * slot], axis=1)
    packed = packed.reshape(columns, tok, width + LANES)
    summed = lax.psum_scatter(packed, COLUMN, scatter_dimension=0, tiled=True)[0]
    grad_bf = summed[:, :width].astype(jnp.bfloat16)
    token_dg = summed[:, width : width + EXPERTS]
    gate_grad = jnp.sum(onehot * token_dg[:, None, :], axis=2)
    sections = lax.axis_size("pipe")
    handed = lax.ppermute(grad_bf[None], "pipe", [(i, i - 1) for i in range(1, sections)])
    return handed, gate_grad[None]


def solution(mesh):
    pipe, expert = mesh.axis_names
    sections, devices = mesh.devices.shape
    fine = Mesh(
        mesh.devices.reshape(sections, devices // 4, 2, 2), (pipe, "z", "xl", "c")
    )
    inner = ("z", "xl", "c")
    rows = P("pipe", inner, None)
    return jax.shard_map(
        on_device,
        mesh=fine,
        in_specs=(rows, rows, rows, rows, P("pipe", None, inner), rows),
        out_specs=(rows, rows),
        check_vma=False,
    )
```

time: 1400 us -> 407 us (0.29)
  waiting for transfers between devices: 1280 us -> 330 us
  starting transfers between devices: 43.3 us -> 12.3 us
  local copies, waits for them, and re-layouts: 41.7 us -> 26.7 us
    all_to_all x4 -> x0, waiting for transfers between devices: 1280 us -> none  [the longest x1 639 us: on_device(): lax.all_to_all(partial_dx, 'expert', split_axis=0, concat_axis=0, tiled=T...]
    reduce_scatter x0 -> x1, waiting for transfers between devices: none -> 177 us  [on_device(): lax.psum_scatter(packed, COLUMN, scatter_dimension=0, tiled=True)[0]]
    all_gather x0 -> x1, waiting for transfers between devices: none -> 145 us  [on_device(): every = lax.all_gather(block, COLUMN, axis=0, tiled=True)]
    all_to_all x4 -> x0, starting transfers between devices: 40.6 us -> none  [the longest x1 17.4 us: on_device(): lax.all_to_all(sent_in, 'expert', split_axis=0, concat_axis=0, tiled=True)]
  transfers between devices with their start and end apart: 5 -> 7, of which waited for: 5 -> 6; matrix products, arithmetic and copies ran while one was open for 2% -> 4% of each run, Pallas kernels for 0% -> 0%
where the time goes in v1:
time: 407 us; the launch traced here: 406 us
  waiting for transfers between devices  330 us (81%)
  local copies, waits for them, and re-layouts  26.7 us (7%)
  between operations  14.2 us (3%)
  matrix products  12.6 us (3%)
  starting transfers between devices  12.3 us (3%)
  other arithmetic  9.85 us (2%)
    reduce_scatter x1, waiting for transfers between devices, on_device(): lax.psum_scatter(packed, COLUMN, scatter_dimension=0, tiled=True)[0]  177 us
    all_gather x1, waiting for transfers between devices, on_device(): every = lax.all_gather(block, COLUMN, axis=0, tiled=True)  145 us
    reshape x1, local copies, waits for them, and re-layouts, on_device(): tails = every.reshape(columns, 2, tok, -1)[..., width:]  9.38 us
    dot_general x1, matrix products, on_device(): lax.dot_general(every[:, :width], weights, (((1,), (1,)), ((), ())), pref...  8.88 us
  transfers between devices with their start and end apart: 7, of which 6 were waited for; matrix products, arithmetic and copies ran while one was open for 4% of the time, Pallas kernels for 0%

profile of v1, /device:TPU:24, one launch (start us, length us, event | category | flops | bytes accessed | tf_op | source)
XLA Modules:
  0.0 406.2 jit_solution(4597673921309400128)
XLA Ops:
  7.2 0.0 all-gather.2.cloned.1.call-start
  7.2 0.8 copy.14
  8.0 0.8 copy.15
  8.8 0.1 select_reduce_fusion.1
  8.9 0.1 fusion.12
  9.0 1.0 select_bitcast_fusion.1
  10.0 1.9 collective-permute-start
  11.9 1.3 collective-permute-done
  13.2 0.7 pad_maximum_fusion.4
  14.0 0.0 all-gather.2.cloned.1.call-update
  14.0 0.0 reduce-scatter.2.cloned.1.call-start
  14.0 2.8 copy.16
  16.8 2.1 collective-permute-start.1
  18.9 3.5 collective-permute-start.2
  22.4 0.1 collective-permute-done.1
  22.5 2.0 broadcast_select_fusion.1
  24.5 0.5 collective-permute-done.2
  25.0 144.9 %all-gather.2.cloned.1.call-done = bf16[768,3712]{1,0:T(8,128)(2,1)} async-done(((bf16[24,3712]{1,0:T(8,128)(2,1)}), bf16[768,3712]{1,0:T(8,128)(2,1)}) %all-gather.2.cloned.1.call-update) | async-done | bytes 5701648 | tf_op jit(solution)/shard_map/all_gather | solution.py:45
  169.9 8.9 %fusion = f32[768,512]{1,0:T(8,128)} fusion(bf16[768,3712]{1,0:T(8,128)(2,1)} %all-gather.2.cloned.1.call-done, bf16[256,3584]{1,0:T(8,128)(2,1)} %bitcast.23, bf16[256,3584]{1,0:T(8,128)(2,1)} %collective-permute-done.2, pred[]{:T(512)S(6)} %eq.38, bf16[256,3584]{1,0:T(8,128)(2,1)} %get-tuple-element.3, bf16[256,3584]{1,0:T(8,128)(2,1)} %get-tuple-element.2), kind=kOutput, calls=%fused_computation.2 | convolution fusion | flops 2835087360 | bytes 14417921 | tf_op jit(solution)/shard_map/dot_general | solution.py:56
  178.8 1.4 reshape.63
  180.2 1.3 slice_select_fusion
  181.5 1.3 select_n.119
  182.8 1.9 collective-permute-start.3
  184.8 0.1 select_n.121
  184.9 9.4 %reshape.64 = bf16[32,2,12,3712]{3,2,1,0:T(8,128)(2,1)} reshape(bf16[768,3712]{1,0:T(8,128)(2,1)} %all-gather.2.cloned.1.call-done) | data formatting | bytes 11403264 | tf_op jit(solution)/shard_map/reshape | solution.py:70
  194.3 1.1 multiply_reduce_fusion.1
  195.4 0.1 mul.73
  195.5 0.0 collective-permute-done.3
  195.5 0.3 multiply_reduce_fusion
  195.8 0.1 broadcast_multiply_fusion
  196.0 3.8 convolution_multiply_fusion
  199.7 2.9 pad_maximum_fusion
  202.6 7.1 %reshape.65 = f32[32,12,3712]{2,1,0:T(8,128)} reshape(f32[384,3712]{1,0:T(8,128)} %pad_maximum_fusion) | data formatting | bytes 11403264 | tf_op jit(solution)/shard_map/reshape | solution.py:79
  209.7 0.0 reduce-scatter.2.cloned.1.call-update
  209.7 177.0 %reduce-scatter.2.cloned.1.call-done = f32[1,12,3712]{2,1,0:T(8,128)} async-done(((f32[32,12,3712]{2,1,0:T(8,128)}), f32[1,12,3712]{2,1,0:T(8,128)}) %reduce-scatter.2.cloned.1.call-update) | async-done | bytes 178192 | tf_op jit(solution)/shard_map/reduce_scatter | solution.py:80
  386.7 1.0 fusion.6
  387.7 0.7 slice.40
  388.4 2.8 collective-permute-start.4
  391.2 0.2 select_reduce_fusion
  391.4 0.7 copy.17
  392.0 6.6 %collective-permute-done.4 = bf16[1,12,3584]{2,1,0:T(8,128)(2,1)S(1)} collective-permute-done((bf16[1,12,3584]{2,1,0:T(8,128)(2,1)S(1)}, bf16[1,12,3584]{2,1,0:T(8,128)(2,1)S(1)}, u32[]{:S(2)}, u32[]{:S(2)}) %collective-permute-start.4) | collective-permute-done | bytes 86048 | tf_op jit(solution)/shard_map/ppermute | solution.py:85
  398.7 0.6 copy.19
  (5 shorter events, 0.1 us)
Async XLA Ops:
  7.2 162.7 %all-gather.2.cloned.1.call-start = ((), (), s32[]{:S(2)}) async-start(), calls=%async_computation.1 | async-start | bytes 5879808 | tf_op jit(solution)/shard_map/all_gather | solution.py:45
  10.0 3.2 collective-permute-start
  14.0 372.7 %reduce-scatter.2.cloned.1.call-start = ((), (), s32[]{:S(2)}) async-start(), calls=%async_computation.2 | async-start | bytes 7839744 | tf_op jit(solution)/shard_map/reduce_scatter | solution.py:80
  16.8 5.7 %collective-permute-start.1 = (bf16[256,3584]{1,0:T(8,128)(2,1)S(1)}, bf16[256,3584]{1,0:T(8,128)(2,1)S(1)}, u32[]{:S(2)}, u32[]{:S(2)}) collective-permute-start(bf16[256,3584]{1,0:T(8,128)(2,1)S(1)} %bitcast.16), channel_id=1, source_target_pairs={{0,1},{1,0},{2,3},{3,2},{4,5},{5,4},{6,7},{7,6},{8,9},{9,8},{10,11... | collective-permute-start | bytes 5505032 | tf_op jit(solution)/shard_map/ppermute | solution.py:13
  18.9 6.1 %collective-permute-start.2 = (bf16[256,3584]{1,0:T(8,128)(2,1)}, bf16[256,3584]{1,0:T(8,128)(2,1)}, u32[]{:S(2)}, u32[]{:S(2)}) collective-permute-start(bf16[256,3584]{1,0:T(8,128)(2,1)} %bitcast.22), channel_id=1, source_target_pairs={{0,1},{2,3},{4,5},{6,7},{8,9},{10,11},{12,13},{14,15},{16,17},{18,... | collective-permute-start | bytes 5505032 | tf_op jit(solution)/shard_map/ppermute | solution.py:52
  182.8 12.7 %collective-permute-start.3 = (f32[384,512]{1,0:T(8,128)S(1)}, f32[384,512]{1,0:T(8,128)S(1)}, u32[]{:S(2)}, u32[]{:S(2)}) collective-permute-start(f32[384,512]{1,0:T(8,128)S(1)} %select_n.119), channel_id=1, source_target_pairs={{0,1},{1,0},{2,3},{3,2},{4,5},{5,4},{6,7},{7,6},{8,9},{9,8},{10,11... | collective-permute-start | bytes 2359304 | tf_op jit(solution)/shard_map/ppermute | solution.py:13
  388.4 10.3 %collective-permute-start.4 = (bf16[1,12,3584]{2,1,0:T(8,128)(2,1)S(1)}, bf16[1,12,3584]{2,1,0:T(8,128)(2,1)S(1)}, u32[]{:S(2)}, u32[]{:S(2)}) collective-permute-start(bf16[1,12,3584]{2,1,0:T(8,128)(2,1)S(1)} %fusion.6), channel_id=1, source_target_pairs={{64,0},{128,64},{192,128},{256,192},{320,256},{384,320},{448,384},... | collective-permute-start | bytes 258056 | tf_op jit(solution)/shard_map/ppermute | solution.py:85
Sparse Core Ops, SparseCore 0:
  14.1 155.7 all-gather.1
  209.8 176.8 reduce-scatter.1
